TPU v7x, 256 devices: a whole 4x4x8 slice. The times are simulated.
256 devices in a mesh: section: 2 (over core), req: 16 (over x, y), head: 8 (over z).
Axes of the slice: x: 4, y: 4, z: 8, core: 2. Of those that a mesh axis runs over, the one named last changes fastest.
Arguments:
- tokens: bfloat16 [256, 8192], P(None, 'req'), may hold values from -14 to 14
- attention_gain: bfloat16 [2, 8192], P('section', 'req'), may hold values from 0.099609375 to 1.8984375
- query_key_value_weight: bfloat16 [2, 8192, 8, 1280], P('section', 'req', 'head'), may hold values from -0.0625 to 0.0625
- head_output_weight: bfloat16 [2, 8, 1024, 8192], P('section', 'head', None, 'req'), may hold values from -0.0625 to 0.0625
- feedforward_gain: bfloat16 [2, 8192], P('section', 'req'), may hold values from 0.099609375 to 1.8984375
- gate_up: bfloat16 [2, 8192, 2, 14336], P('section', 'req', None, 'head'), may hold values from -0.0625 to 0.0625
- down_weight: bfloat16 [2, 14336, 8192], P('section', 'head', 'req'), may hold values from -0.046875 to 0.046875
- packed_cache: bfloat16 [2, 32768, 8, 256], P('section', 'req', 'head'), may hold values from -70 to 70
- long_cache: bfloat16 [2, 2, 32768, 8, 256], P('section', None, 'req', 'head'), may hold values from -70 to 70
- lengths: int32 [16, 16], P('req'), may hold values from 1 to 256, 2048 in all within a row
- long_split: int32 [2, 16], P(None, 'req'), may hold values from 1 to 2048, 16384 in all within a row
Outputs:
- layer_outputs: bfloat16 [2, 256, 8192], P('section', None, 'req')
Inputs may be any that keep to these rules, and one draw needn't show every extreme that they name: Row g holds the lengths of the 16 requests of request group g in order; they sum to 2048, and the requests' keys fill that group's 2048 slots of packed_cache one request after another. `long_split`: entry (j, g) counts the live slots, the first ones, of group g's 2048 slots of long request j; each row sums to 16384.
All inputs are finite; a program needn't handle non-finite values.
Results may differ from a plain program's by a relative error of at most 0.04.
Values may be sent and summed in bfloat16 or wider, within the bound.
A program may use at most 64 MiB of HBM per device.

v0:
```python
import math
import jax
import jax.numpy as jnp
from jax import lax
from jax.sharding import PartitionSpec as P

MODEL_WIDTH = 8192
QUERY_HEADS = 64
KEY_VALUE_HEADS = 8
HEAD_SIZE = 128
LONG = 16384
EPSILON = 1e-05


def merged(part, axis, combine):
    gathered = jax.tree.map(lambda a: lax.all_gather(a, axis), part)

    def take(source):
        return jax.tree.map(lambda a: lax.dynamic_index_in_dim(a, source, 0, False), gathered)

    return lax.fori_loop(
        1, lax.axis_size(axis), lambda source, state: combine(state, take(source)), take(0)
    )


def shifted(value, axis, by):
    peers = lax.axis_size(axis)
    pairs = [(i, i + by) for i in range(peers) if 0 <= i + by < peers]
    return lax.ppermute(value, axis, pairs)


def rotate(values, position):
    half_dim = values.shape[-1] // 2
    freq_ids = jnp.arange(half_dim).astype(jnp.float32)
    inverse = 1.0 / 10000.0 ** (freq_ids * 2.0 / values.shape[-1])
    angles = position.astype(jnp.float32)[:, None] * inverse[None, :]
    cosine = jnp.cos(angles)[:, None, None, :]
    sine_part = jnp.sin(angles)[:, None, None, :]
    lower_half = values[..., :half_dim]
    upper_half = values[..., half_dim:]
    return jnp.concatenate(
        [
            lower_half * cosine - upper_half * sine_part,
            upper_half * cosine + lower_half * sine_part,
        ],
        -1,
    )


def add_pair(earlier, second_part):
    return earlier + second_part


def combine_partial(earlier, second_part):
    peak = jnp.maximum(earlier[0], second_part[0])
    left_factor = jnp.exp(earlier[0] - peak)
    right_factor = jnp.exp(second_part[0] - peak)
    softmax_total = earlier[1] * left_factor + second_part[1] * right_factor
    weighted_sum = earlier[2] * left_factor[..., None] + second_part[2] * right_factor[..., None]
    return (peak, softmax_total, weighted_sum)


def over_requests(values, combiner):
    return merged(values, "req", combiner)


def rows_apply(values, row_fn):
    return row_fn(lax.all_gather(values, "req", axis=0, tiled=True), jnp.int32(0))


def rows_project(term_fn, row_count):
    return lax.psum_scatter(
        term_fn(jnp.int32(0), row_count * lax.axis_size("req")),
        "req",
        scatter_dimension=0,
        tiled=True,
    )


def head_total(values):
    return lax.psum(values, "head")


def keep_rows(piece_rows, start_row):
    return piece_rows


def norm_rows(values, gain_row):
    floats = values.astype(jnp.float32)
    squares = over_requests(jnp.sum(floats * floats, axis=-1), add_pair)
    return (
        floats * lax.rsqrt(squares / MODEL_WIDTH + EPSILON)[:, None] * gain_row.astype(jnp.float32)
    ).astype(jnp.bfloat16)


def decoder_layer(
    inputs,
    micro_batch,
    attention_gain,
    query_key_value_weight,
    head_output_weight,
    feedforward_gain,
    gate_up,
    down_weight,
    packed_cache,
    long_cache,
    lengths,
    long_split,
):
    req_count = lax.axis_size("req")
    group_index = lax.axis_index("req")
    blocks = inputs.shape[0] // req_count
    columns = query_key_value_weight.shape[1]
    kv_local = query_key_value_weight.shape[2]
    requests_per_group = QUERY_HEADS // KEY_VALUE_HEADS
    score_scale = 1.0 / math.sqrt(HEAD_SIZE)
    normalized_input = norm_rows(inputs, attention_gain[0])
    in_weights = query_key_value_weight[0].reshape(
        columns, kv_local * (requests_per_group + 2) * HEAD_SIZE
    )

    def qkv_term(start_row, row_count):
        return jnp.dot(normalized_input, in_weights, preferred_element_type=jnp.float32)

    projected_rows = rows_project(qkv_term, blocks).reshape(
        blocks, kv_local, requests_per_group + 2, HEAD_SIZE
    )
    local_rows = jnp.arange(blocks)
    row_lengths = lengths[0]
    owner_long = (group_index == 0) | (group_index == req_count // 2)
    long_row = (local_rows == 0) & (micro_batch == 0) & owner_long
    position = row_lengths + jnp.where(long_row, LONG, 0).astype(jnp.int32)
    queries = rotate(projected_rows[:, :, :requests_per_group], position).astype(jnp.bfloat16)
    new_key = rotate(projected_rows[:, :, requests_per_group : requests_per_group + 1], position)[
        :, :, 0
    ].astype(jnp.bfloat16)
    new_value = projected_rows[:, :, requests_per_group + 1].astype(jnp.bfloat16)
    gathered = rows_apply(
        queries[0:1].reshape(1, kv_local * requests_per_group * HEAD_SIZE), keep_rows
    )
    long_queries = jnp.stack([gathered[0], gathered[req_count // 2]]).reshape(
        2, kv_local, requests_per_group, HEAD_SIZE
    )
    far_cache = long_cache[0]
    far_live = (jnp.arange(far_cache.shape[1])[None, :] < long_split[:, 0][:, None])[
        :, None, None, :
    ]
    far_scores = (
        jnp.einsum(
            "jkhd,jpkd->jkhp",
            long_queries,
            far_cache[..., :HEAD_SIZE],
            preferred_element_type=jnp.float32,
        )
        * score_scale
    )
    far_max = jnp.max(jnp.where(far_live, far_scores, -jnp.inf), axis=-1)
    far_weights = jnp.where(
        far_live, jnp.exp(jnp.where(far_live, far_scores - far_max[..., None], 0.0)), 0.0
    ).astype(jnp.bfloat16)
    far_totals = jnp.sum(far_weights.astype(jnp.float32), axis=-1)
    far_summed = jnp.einsum(
        "jkhp,jpkd->jkhd",
        far_weights,
        far_cache[..., HEAD_SIZE:],
        preferred_element_type=jnp.float32,
    )
    far_max, far_totals, far_summed = over_requests(
        (far_max, far_totals, far_summed), combine_partial
    )
    far_index = jnp.where(group_index == 0, 0, 1)
    chosen_max = lax.dynamic_index_in_dim(far_max, far_index, 0, keepdims=False)
    chosen_totals = lax.dynamic_index_in_dim(far_totals, far_index, 0, keepdims=False)
    chosen_summed = lax.dynamic_index_in_dim(far_summed, far_index, 0, keepdims=False)
    pack_part = packed_cache[0]
    seg_ends = jnp.cumsum(lengths[0])
    slot_ids = jnp.arange(pack_part.shape[0])
    slot_owner = jnp.sum((slot_ids[:, None] >= seg_ends[None, :]).astype(jnp.int32), axis=1)
    request_ids = micro_batch * blocks + local_rows
    in_segment = (slot_owner[None, :] == request_ids[:, None])[:, None, None, :]
    scores = (
        jnp.einsum(
            "rkhd,pkd->rkhp",
            queries,
            pack_part[..., :HEAD_SIZE],
            preferred_element_type=jnp.float32,
        )
        * score_scale
    )
    own_score = (
        jnp.einsum("rkhd,rkd->rkh", queries, new_key, preferred_element_type=jnp.float32)
        * score_scale
    )
    row_max = jnp.maximum(jnp.max(jnp.where(in_segment, scores, -jnp.inf), axis=-1), own_score)
    long_mask = long_row[:, None, None]
    row_max = jnp.where(long_mask, jnp.maximum(row_max, chosen_max[None]), row_max)
    weights = jnp.where(
        in_segment, jnp.exp(jnp.where(in_segment, scores - row_max[..., None], 0.0)), 0.0
    ).astype(jnp.bfloat16)
    own_weights = jnp.exp(own_score - row_max).astype(jnp.bfloat16)
    far_factor = jnp.where(
        long_mask, jnp.exp(jnp.where(long_mask, chosen_max[None] - row_max, 0.0)), 0.0
    )
    softmax_total = (
        jnp.sum(weights.astype(jnp.float32), axis=-1)
        + own_weights.astype(jnp.float32)
        + far_factor * chosen_totals[None]
    )
    weighted_sum = jnp.einsum(
        "rkhp,pkd->rkhd", weights, pack_part[..., HEAD_SIZE:], preferred_element_type=jnp.float32
    )
    weighted_sum = (
        weighted_sum
        + own_weights.astype(jnp.float32)[..., None] * new_value.astype(jnp.float32)[:, :, None, :]
    )
    weighted_sum = weighted_sum + far_factor[..., None] * chosen_summed[None]
    attended_heads = (
        (weighted_sum / softmax_total[..., None])
        .astype(jnp.bfloat16)
        .reshape(blocks, kv_local * requests_per_group * HEAD_SIZE)
    )
    out_weights = head_output_weight[0].reshape(kv_local * requests_per_group * HEAD_SIZE, columns)

    def project_heads(piece_rows, start_row):
        return jnp.dot(piece_rows, out_weights, preferred_element_type=jnp.float32)

    attended = head_total(rows_apply(attended_heads, project_heads))
    residual = (inputs.astype(jnp.float32) + attended).astype(jnp.bfloat16)
    normed_two = norm_rows(residual, feedforward_gain[0])
    ff_weights = gate_up[0].reshape(columns, -1)

    def ff_term(start_row, row_count):
        return jnp.dot(normed_two, ff_weights, preferred_element_type=jnp.float32)

    gate_and_up = rows_project(ff_term, blocks)
    hidden_width = gate_and_up.shape[1] // 2
    hidden = (jax.nn.silu(gate_and_up[:, :hidden_width]) * gate_and_up[:, hidden_width:]).astype(
        jnp.bfloat16
    )
    lower_weights = down_weight[0]

    def project_hidden(piece_rows, start_row):
        return jnp.dot(piece_rows, lower_weights, preferred_element_type=jnp.float32)

    lowered = head_total(rows_apply(hidden, project_hidden))
    return (residual.astype(jnp.float32) + lowered).astype(jnp.bfloat16)


def local(
    tokens,
    attention_gain,
    query_key_value_weight,
    head_output_weight,
    feedforward_gain,
    gate_up,
    down_weight,
    packed_cache,
    long_cache,
    lengths,
    long_split,
):
    req_count = lax.axis_size("req")
    section_index = lax.axis_index("section")
    batch_count = 1
    per_group = tokens.shape[0] // req_count
    blocks = per_group // batch_count
    columns = tokens.shape[1]
    token_grid = tokens.reshape(req_count, per_group, columns)
    result = jnp.zeros_like(token_grid)
    incoming = jnp.zeros((req_count * blocks, columns), jnp.bfloat16)
    for phase_step in range(batch_count + 1):
        micro_batch = phase_step - section_index
        is_active = (micro_batch >= 0) & (micro_batch < batch_count)
        micro_batch = jnp.clip(micro_batch, 0, batch_count - 1)
        new_batch = token_grid.reshape(req_count * blocks, columns)
        inputs = jnp.where(section_index == 0, new_batch, incoming)
        output = decoder_layer(
            inputs,
            micro_batch,
            attention_gain,
            query_key_value_weight,
            head_output_weight,
            feedforward_gain,
            gate_up,
            down_weight,
            packed_cache,
            long_cache,
            lengths,
            long_split,
        )
        placed = output.reshape(req_count, blocks, columns)
        result = jnp.where(is_active, placed, result)
        if phase_step < batch_count:
            incoming = shifted(output, "section", 1)
    return result.reshape(1, req_count * per_group, columns)


def solution(mesh):
    placed = (
        P(None, "req"),
        P("section", "req"),
        P("section", "req", "head", None),
        P("section", "head", None, "req"),
        P("section", "req"),
        P("section", "req", None, "head"),
        P("section", "head", "req"),
        P("section", "req", "head", None),
        P("section", None, "req", "head", None),
        P("req", None),
        P(None, "req"),
    )
    return jax.shard_map(
        local, mesh=mesh, in_specs=placed, out_specs=P("section", None, "req"), check_vma=False
    )
```

profile of v0, /device:TPU:2, one launch (start us, length us, event | category | flops | bytes accessed | tf_op | source)
XLA Modules:
  0.0 1032.9 jit_solution(9253363095233518662)
XLA Ops:
  6.5 1.2 fusion.34
  7.8 23.3 %all-gather.10 = f32[16,1,256]{2,1,0:T(1,128)S(1)} all-gather(f32[1,1,256]{2,1,0:T(1,128)S(1)} %bitcast.379), channel_id=2, replica_groups=mesh['section'=2,'req'=16,'head'=8] {'req'}, dimensions={0}, use_global_device_ids=true | all-gather | bytes 17408 | tf_op jit(solution)/shard_map/all_gather | solution.py:16
  32.5 3.0 fusion.18
  36.4 78.1 %reduce-scatter.5.cloned.1.call-done = f32[16,1280]{1,0:T(8,128)} async-done(((f32[256,1280]{1,0:T(8,128)}), f32[16,1280]{1,0:T(8,128)}) %reduce-scatter.5.cloned.1.call-update) | async-done | bytes 81936 | tf_op jit(solution)/shard_map/reduce_scatter | solution.py:72
  115.7 21.4 %all-gather.11 = bf16[16,1,1024]{2,1,0:T(2,128)(2,1)S(1)} all-gather(bf16[1,1,1024]{2,1,0:T(2,128)(2,1)S(1)} %reshape.774), channel_id=1, replica_groups=mesh['section'=2,'req'=16,'head'=8] {'req'}, dimensions={0}, use_global_device_ids=true | all-gather | bytes 34816 | tf_op jit(solution)/shard_map/all_gather | solution.py:68
  137.2 1.7 select_reduce_fusion.3
  139.1 1.5 fusion.33
  140.6 22.6 %all-gather.12 = f32[16,2,8]{2,1,0:T(2,128)S(1)} all-gather(f32[1,2,8]{2,1,0:T(2,128)S(1)} %bitcast.371), channel_id=3, replica_groups=mesh['section'=2,'req'=16,'head'=8] {'req'}, dimensions={0}, use_global_device_ids=true | all-gather | bytes 1088 | tf_op jit(solution)/shard_map/all_gather | solution.py:16
  163.2 21.1 %all-gather.13 = f32[16,2,8]{2,1,0:T(2,128)S(1)} all-gather(f32[1,2,8]{2,1,0:T(2,128)S(1)} %bitcast.375), channel_id=4, replica_groups=mesh['section'=2,'req'=16,'head'=8] {'req'}, dimensions={0}, use_global_device_ids=true | all-gather | bytes 1088 | tf_op jit(solution)/shard_map/all_gather | solution.py:16
  184.3 23.0 %all-gather.3 = f32[32,8,128]{2,1,0:T(8,128)S(1)} all-gather(f32[2,8,128]{2,1,0:T(8,128)S(1)} %fusion.33), channel_id=5, replica_groups=mesh['section'=2,'req'=16,'head'=8] {'req'}, dimensions={0}, use_global_device_ids=true | all-gather | bytes 139264 | tf_op jit(solution)/shard_map/all_gather | solution.py:16
  207.4 1.7 while.99
  211.0 21.7 %all_gather.87 = bf16[256,1024]{1,0:T(8,128)(2,1)S(1)} all-gather(bf16[16,1024]{1,0:T(8,128)(2,1)S(1)} %bitcast.340), channel_id=1, replica_groups=mesh['section'=2,'req'=16,'head'=8] {'req'}, dimensions={0}, use_global_device_ids=true | all-gather | bytes 557056 | tf_op jit(solution)/shard_map/all_gather | solution.py:68
  232.7 1.3 fusion.30
  234.1 4.5 copy.75
  238.6 69.5 %all-reduce.5.cloned.1.call-done = f32[256,512]{1,0:T(8,128)} async-done(((f32[256,512]{1,0:T(8,128)}), f32[256,512]{1,0:T(8,128)}) %all-reduce.5.cloned.1.call-update) | async-done | bytes 524304 | tf_op jit(solution)/shard_map/psum | solution.py:81
  308.0 1.2 fusion.38
  309.3 23.0 %all-gather.14 = f32[16,1,256]{2,1,0:T(1,128)S(1)} all-gather(f32[1,1,256]{2,1,0:T(1,128)S(1)} %bitcast.378), channel_id=6, replica_groups=mesh['section'=2,'req'=16,'head'=8] {'req'}, dimensions={0}, use_global_device_ids=true | all-gather | bytes 17408 | tf_op jit(solution)/shard_map/all_gather | solution.py:16
  333.0 5.0 fusion.57
  338.1 77.9 %reduce-scatter.7.cloned.1.call-done = f32[16,3584]{1,0:T(8,128)} async-done(((f32[256,3584]{1,0:T(8,128)}), f32[16,3584]{1,0:T(8,128)}) %reduce-scatter.7.cloned.1.call-update) | async-done | bytes 229392 | tf_op jit(solution)/shard_map/reduce_scatter | solution.py:72
  416.0 1.0 fusion.70
  417.0 23.0 %all_gather.90 = bf16[256,1792]{1,0:T(8,128)(2,1)S(1)} all-gather(bf16[16,1792]{1,0:T(8,128)(2,1)S(1)} %fusion.70), channel_id=1, replica_groups=mesh['section'=2,'req'=16,'head'=8] {'req'}, dimensions={0}, use_global_device_ids=true | all-gather | bytes 974848 | tf_op jit(solution)/shard_map/all_gather | solution.py:68
  440.1 1.4 fusion.14
  441.6 73.4 %all-reduce.7.cloned.1.call-done = f32[256,512]{1,0:T(8,128)} async-done(((f32[256,512]{1,0:T(8,128)}), f32[256,512]{1,0:T(8,128)}) %all-reduce.7.cloned.1.call-update) | async-done | bytes 524304 | tf_op jit(solution)/shard_map/psum | solution.py:81
  515.0 1.9 fusion.41
  516.9 2.0 collective-permute-start
  520.5 23.0 %all-gather.15 = f32[16,1,256]{2,1,0:T(1,128)S(1)} all-gather(f32[1,1,256]{2,1,0:T(1,128)S(1)} %bitcast.376), channel_id=7, replica_groups=mesh['section'=2,'req'=16,'head'=8] {'req'}, dimensions={0}, use_global_device_ids=true | all-gather | bytes 17408 | tf_op jit(solution)/shard_map/all_gather | solution.py:16
  544.2 2.6 fusion.16
  546.8 74.6 %reduce-scatter.9.cloned.1.call-done = f32[16,1280]{1,0:T(8,128)} async-done(((f32[256,1280]{1,0:T(8,128)}), f32[16,1280]{1,0:T(8,128)}) %reduce-scatter.9.cloned.1.call-update) | async-done | bytes 81936 | tf_op jit(solution)/shard_map/reduce_scatter | solution.py:72
  622.6 21.5 %all-gather.16 = bf16[16,1,1024]{2,1,0:T(2,128)(2,1)S(1)} all-gather(bf16[1,1,1024]{2,1,0:T(2,128)(2,1)S(1)} %reshape.784), channel_id=1, replica_groups=mesh['section'=2,'req'=16,'head'=8] {'req'}, dimensions={0}, use_global_device_ids=true | all-gather | bytes 34816 | tf_op jit(solution)/shard_map/all_gather | solution.py:68
  644.1 1.7 select_reduce_fusion.2
  646.0 1.5 fusion.32
  647.7 1.5 select_reduce_fusion
  649.5 22.6 %all-gather.17 = f32[16,2,8]{2,1,0:T(2,128)S(1)} all-gather(f32[1,2,8]{2,1,0:T(2,128)S(1)} %bitcast.370), channel_id=8, replica_groups=mesh['section'=2,'req'=16,'head'=8] {'req'}, dimensions={0}, use_global_device_ids=true | all-gather | bytes 1088 | tf_op jit(solution)/shard_map/all_gather | solution.py:16
  672.1 21.1 %all-gather.18 = f32[16,2,8]{2,1,0:T(2,128)S(1)} all-gather(f32[1,2,8]{2,1,0:T(2,128)S(1)} %bitcast.374), channel_id=9, replica_groups=mesh['section'=2,'req'=16,'head'=8] {'req'}, dimensions={0}, use_global_device_ids=true | all-gather | bytes 1088 | tf_op jit(solution)/shard_map/all_gather | solution.py:16
  693.2 22.9 %all-gather.8 = f32[32,8,128]{2,1,0:T(8,128)S(1)} all-gather(f32[2,8,128]{2,1,0:T(8,128)S(1)} %fusion.32), channel_id=10, replica_groups=mesh['section'=2,'req'=16,'head'=8] {'req'}, dimensions={0}, use_global_device_ids=true | all-gather | bytes 139264 | tf_op jit(solution)/shard_map/all_gather | solution.py:16
  716.1 1.7 while.102
  718.4 1.5 fusion.26
  719.9 22.1 %all_gather.100 = bf16[256,1024]{1,0:T(8,128)(2,1)S(1)} all-gather(bf16[16,1024]{1,0:T(8,128)(2,1)S(1)} %bitcast.341), channel_id=1, replica_groups=mesh['section'=2,'req'=16,'head'=8] {'req'}, dimensions={0}, use_global_device_ids=true | all-gather | bytes 557056 | tf_op jit(solution)/shard_map/all_gather | solution.py:68
  742.0 1.2 fusion.28
  743.4 73.8 %all-reduce.9.cloned.1.call-done = f32[256,512]{1,0:T(8,128)} async-done(((f32[256,512]{1,0:T(8,128)}), f32[256,512]{1,0:T(8,128)}) %all-reduce.9.cloned.1.call-update) | async-done | bytes 524304 | tf_op jit(solution)/shard_map/psum | solution.py:81
  817.2 1.2 fusion.46
  818.4 23.0 %all-gather.19 = f32[16,1,256]{2,1,0:T(1,128)S(1)} all-gather(f32[1,1,256]{2,1,0:T(1,128)S(1)} %bitcast.377), channel_id=11, replica_groups=mesh['section'=2,'req'=16,'head'=8] {'req'}, dimensions={0}, use_global_device_ids=true | all-gather | bytes 17408 | tf_op jit(solution)/shard_map/all_gather | solution.py:16
  842.1 5.0 fusion.54
  847.2 78.0 %reduce-scatter.11.cloned.1.call-done = f32[16,3584]{1,0:T(8,128)} async-done(((f32[256,3584]{1,0:T(8,128)}), f32[16,3584]{1,0:T(8,128)}) %reduce-scatter.11.cloned.1.call-update) | async-done | bytes 229392 | tf_op jit(solution)/shard_map/reduce_scatter | solution.py:72
  926.2 23.0 %all_gather.103 = bf16[256,1792]{1,0:T(8,128)(2,1)S(1)} all-gather(bf16[16,1792]{1,0:T(8,128)(2,1)S(1)} %fusion.69), channel_id=1, replica_groups=mesh['section'=2,'req'=16,'head'=8] {'req'}, dimensions={0}, use_global_device_ids=true | all-gather | bytes 974848 | tf_op jit(solution)/shard_map/all_gather | solution.py:68
  949.2 1.5 fusion.12
  950.7 73.4 %all-reduce.11.cloned.1.call-done = f32[256,512]{1,0:T(8,128)} async-done(((f32[256,512]{1,0:T(8,128)}), f32[256,512]{1,0:T(8,128)}) %all-reduce.11.cloned.1.call-update) | async-done | bytes 524304 | tf_op jit(solution)/shard_map/psum | solution.py:81
  1024.1 1.9 fusion.53
  (354 shorter events, 17.5 us)
Async XLA Ops:
  6.5 433.5 %copy-start = (bf16[1,1792,512]{2,1,0:T(8,128)(2,1)S(1)}, bf16[1,1792,512]{2,1,0:T(8,128)(2,1)}, u32[]{:S(2)}) copy-start(bf16[1,1792,512]{2,1,0:T(8,128)(2,1)} %param.29) | copy-start | bytes 5505028
  6.5 108.0 %reduce-scatter.5.cloned.1.call-start = ((), (), s32[]{:S(2)}) async-start(), calls=%async_computation.4 | async-start | bytes 1392640 | tf_op jit(solution)/shard_map/reduce_scatter | solution.py:72
  32.5 3.2 copy-start.9
  32.5 3.7 copy-start.10
  35.6 272.5 %all-reduce.5.cloned.1.call-start = ((), (), s32[]{:S(2)}) async-start(), calls=%async_computation.5 | async-start | bytes 1048576 | tf_op jit(solution)/shard_map/psum | solution.py:81
  35.9 173.5 %copy-start.7 = (bf16[1,2048,1,256]{3,1,2,0:T(8,128)(2,1)S(1)}, bf16[1,2048,1,256]{3,1,2,0:T(8,128)(2,1)}, u32[]{:S(2)}) copy-start(bf16[1,2048,1,256]{3,1,2,0:T(8,128)(2,1)} %param.30) | copy-start | bytes 3145732
  210.1 22.7 %copy-start.3 = (bf16[1,1,1024,512]{3,2,1,0:T(8,128)(2,1)S(1)}, bf16[1,1,1024,512]{3,2,1,0:T(8,128)(2,1)}, u32[]{:S(2)}) copy-start(bf16[1,1,1024,512]{3,2,1,0:T(8,128)(2,1)} %param.26) | copy-start | bytes 3145732
  234.0 182.0 %reduce-scatter.7.cloned.1.call-start = ((), (), s32[]{:S(2)}) async-start(), calls=%async_computation.6 | async-start | bytes 3899392 | tf_op jit(solution)/shard_map/reduce_scatter | solution.py:72
  234.1 4.5 copy-start.8
  234.1 74.0 %copy-start.2 = (bf16[256,512]{1,0:T(8,128)(2,1)S(1)}, bf16[256,512]{1,0:T(8,128)(2,1)}, u32[]{:S(2)}) copy-start(bf16[256,512]{1,0:T(8,128)(2,1)} %param.23) | copy-start | bytes 786436
  309.3 28.8 %copy-start.5 = (bf16[256,512]{1,0:T(8,128)(2,1)}, bf16[256,512]{1,0:T(8,128)(2,1)S(1)}, u32[]{:S(2)}) copy-start(bf16[256,512]{1,0:T(8,128)(2,1)S(1)} %get-tuple-element.859) | copy-start | bytes 786436
  338.1 176.9 %all-reduce.7.cloned.1.call-start = ((), (), s32[]{:S(2)}) async-start(), calls=%async_computation.7 | async-start | bytes 1048576 | tf_op jit(solution)/shard_map/psum | solution.py:81
  441.5 102.7 %copy-start.1 = (bf16[1,512,1,1280]{3,1,2,0:T(8,128)(2,1)S(1)}, bf16[1,512,1,1280]{3,1,2,0:T(8,128)(2,1)}, u32[]{:S(2)}) copy-start(bf16[1,512,1,1280]{3,1,2,0:T(8,128)(2,1)} %param.25) | copy-start | bytes 3932164
  441.5 179.9 %reduce-scatter.9.cloned.1.call-start = ((), (), s32[]{:S(2)}) async-start(), calls=%async_computation.8 | async-start | bytes 1392640 | tf_op jit(solution)/shard_map/reduce_scatter | solution.py:72
  516.9 2.8 collective-permute-start
  546.8 270.4 %all-reduce.9.cloned.1.call-start = ((), (), s32[]{:S(2)}) async-start(), calls=%async_computation.9 | async-start | bytes 1048576 | tf_op jit(solution)/shard_map/psum | solution.py:81
  717.9 24.1 %copy-start.4 = (bf16[1,1,1024,512]{3,2,1,0:T(8,128)(2,1)S(1)}, bf16[1,1,1024,512]{3,2,1,0:T(8,128)(2,1)}, u32[]{:S(2)}) copy-start(bf16[1,1,1024,512]{3,2,1,0:T(8,128)(2,1)} %param.26) | copy-start | bytes 3145732
  719.9 97.2 %copy-start.6 = (bf16[256,512]{1,0:T(8,128)(2,1)S(1)}, bf16[256,512]{1,0:T(8,128)(2,1)}, u32[]{:S(2)}) copy-start(bf16[256,512]{1,0:T(8,128)(2,1)} %get-tuple-element.857) | copy-start | bytes 786436
  743.3 181.8 %reduce-scatter.11.cloned.1.call-start = ((), (), s32[]{:S(2)}) async-start(), calls=%async_computation.10 | async-start | bytes 3899392 | tf_op jit(solution)/shard_map/reduce_scatter | solution.py:72
  847.2 176.9 %all-reduce.11.cloned.1.call-start = ((), (), s32[]{:S(2)}) async-start(), calls=%async_computation.11 | async-start | bytes 1048576 | tf_op jit(solution)/shard_map/psum | solution.py:81
Sparse Core Ops, SparseCore 0:
  35.7 78.7 reduce-scatter.4
  234.1 73.8 all-reduce.4
  338.2 77.7 reduce-scatter.6
  441.6 73.2 all-reduce.6
  546.9 74.4 reduce-scatter.8
  743.4 73.6 all-reduce.8
  847.3 77.8 reduce-scatter.10
  950.8 73.2 all-reduce.10
where the time goes:
time: 1030 us
  waiting for transfers between devices  600 us (58%)
  blocking collectives  358 us (35%)
  matrix products  31.8 us (3%)
  other arithmetic  17.6 us (2%)
  between operations  13.9 us (1%)
    reduce_scatter x4, waiting for transfers between devices, rows_project(): lax.psum_scatter(term_fn(jnp.int32(0), row_count * lax.axis_size('req')),...  309 us
    psum x4, waiting for transfers between devices, head_total(): return lax.psum(values, 'head')  290 us
    all_gather x10, blocking collectives, merged(): gathered = jax.tree.map(lambda a: lax.all_gather(a, axis), part)  226 us
    all_gather x6, blocking collectives, rows_apply(): lax.all_gather(values, 'req', axis=0, tiled=True)  133 us
  transfers between devices with their start and end apart: 9, of which 9 were waited for; matrix products, arithmetic and copies ran while one was open for 1% of the time, Pallas kernels for 0%

commit v1 on v0

--- a/solution.py
+++ b/solution.py
@@ -10,6 +10,12 @@
 HEAD_SIZE = 128
 LONG = 16384
 EPSILON = 1e-05
+
+
+def gather_from_all(x, axis, dim):
+    length = lax.axis_size(axis)
+    repeats = [length if d == dim else 1 for d in range(x.ndim)]
+    return lax.all_to_all(jnp.tile(x, repeats), axis, split_axis=dim, concat_axis=dim, tiled=True)
 
 
 def merged(part, axis, combine):
@@ -65,7 +71,7 @@
 
 
 def rows_apply(values, row_fn):
-    return row_fn(lax.all_gather(values, "req", axis=0, tiled=True), jnp.int32(0))
+    return row_fn(gather_from_all(values, "req", 0), jnp.int32(0))
 
 
 def rows_project(term_fn, row_count):

time: 1030 us -> 987 us (0.958)
  blocking collectives: 358 us -> 288 us
  starting transfers between devices: 2.28 us -> 13.7 us
    all_gather x6 -> x0, blocking collectives: 133 us -> none  [rows_apply(): lax.all_gather(values, 'req', axis=0, tiled=True)]
    all_to_all x0 -> x4, blocking collectives: none -> 61.2 us  [gather_from_all(): lax.all_to_all(jnp.tile(x, repeats), axis, split_axis=dim, concat_axis=di...]
    all_to_all x0 -> x2, starting transfers between devices: none -> 11.4 us  [gather_from_all(): lax.all_to_all(jnp.tile(x, repeats), axis, split_axis=dim, concat_axis=di...]
  transfers between devices with their start and end apart: 9 -> 11, of which waited for: 9 -> 11; matrix products, arithmetic and copies ran while one was open for 1% -> 1% of each run, Pallas kernels for 0% -> 0%
where the time goes in v1:
time: 987 us; the launch traced here: 986 us
  waiting for transfers between devices  606 us (61%)
  blocking collectives  288 us (29%)
  matrix products  34.1 us (3%)
  other arithmetic  19.3 us (2%)
  between operations  13.9 us (1%)
  starting transfers between devices  13.7 us (1%)
    reduce_scatter x4, waiting for transfers between devices, rows_project(): lax.psum_scatter(term_fn(jnp.int32(0), row_count * lax.axis_size('req')),...  308 us
    psum x4, waiting for transfers between devices, head_total(): return lax.psum(values, 'head')  288 us
    all_gather x10, blocking collectives, merged(): gathered = jax.tree.map(lambda a: lax.all_gather(a, axis), part)  226 us
    all_to_all x4, blocking collectives, gather_from_all(): lax.all_to_all(jnp.tile(x, repeats), axis, split_axis=dim, concat_axis=di...  61.2 us
  transfers between devices with their start and end apart: 11, of which 11 were waited for; matrix products, arithmetic and copies ran while one was open for 1% of the time, Pallas kernels for 0%

profile of v1, /device:TPU:2, one launch (start us, length us, event | category | flops | bytes accessed | tf_op | source)
XLA Modules:
  0.0 986.1 jit_solution(3263592667374714678)
XLA Ops:
  7.8 23.3 %all-gather.10 = f32[16,1,256]{2,1,0:T(1,128)S(1)} all-gather(f32[1,1,256]{2,1,0:T(1,128)S(1)} %bitcast.369), channel_id=2, replica_groups=mesh['section'=2,'req'=16,'head'=8] {'req'}, dimensions={0}, use_global_device_ids=true | all-gather | bytes 17408 | tf_op jit(solution)/shard_map/all_gather | solution.py:22
  32.5 3.0 fusion.18
  36.4 78.2 %reduce-scatter.5.cloned.1.call-done = f32[16,1280]{1,0:T(8,128)} async-done(((f32[256,1280]{1,0:T(8,128)}), f32[16,1280]{1,0:T(8,128)}) %reduce-scatter.5.cloned.1.call-update) | async-done | bytes 81936 | tf_op jit(solution)/shard_map/reduce_scatter | solution.py:78
  117.9 5.7 all-to-all-start
  124.0 1.5 select_reduce_fusion.1
  125.5 4.3 all-to-all-done
  129.9 1.7 select_reduce_fusion.3
  131.8 1.5 fusion.33
  133.3 21.7 %all-gather.11 = f32[16,2,8]{2,1,0:T(2,128)S(1)} all-gather(f32[1,2,8]{2,1,0:T(2,128)S(1)} %bitcast.357), channel_id=3, replica_groups=mesh['section'=2,'req'=16,'head'=8] {'req'}, dimensions={0}, use_global_device_ids=true | all-gather | bytes 1088 | tf_op jit(solution)/shard_map/all_gather | solution.py:22
  155.0 21.4 %all-gather.12 = f32[16,2,8]{2,1,0:T(2,128)S(1)} all-gather(f32[1,2,8]{2,1,0:T(2,128)S(1)} %bitcast.365), channel_id=4, replica_groups=mesh['section'=2,'req'=16,'head'=8] {'req'}, dimensions={0}, use_global_device_ids=true | all-gather | bytes 1088 | tf_op jit(solution)/shard_map/all_gather | solution.py:22
  176.4 23.8 %all-gather.3 = f32[32,8,128]{2,1,0:T(8,128)S(1)} all-gather(f32[2,8,128]{2,1,0:T(8,128)S(1)} %fusion.33), channel_id=5, replica_groups=mesh['section'=2,'req'=16,'head'=8] {'req'}, dimensions={0}, use_global_device_ids=true | all-gather | bytes 139264 | tf_op jit(solution)/shard_map/all_gather | solution.py:22
  200.3 1.7 while.99
  202.6 1.6 fusion.27
  204.2 13.1 %all_to_all.48 = bf16[16,16,1024]{2,1,0:T(8,128)(2,1)S(1)} all-to-all(bf16[16,16,1024]{2,1,0:T(8,128)(2,1)S(1)} %tile.23), channel_id=1, replica_groups=mesh['section'=2,'req'=16,'head'=8] {'req'}, dimensions={0} | all-to-all | bytes 1048576 | tf_op jit(solution)/shard_map/all_to_all | solution.py:18
  217.3 1.2 fusion.30
  218.7 4.5 copy.74
  223.2 68.7 %all-reduce.5.cloned.1.call-done = f32[256,512]{1,0:T(8,128)} async-done(((f32[256,512]{1,0:T(8,128)}), f32[256,512]{1,0:T(8,128)}) %all-reduce.5.cloned.1.call-update) | async-done | bytes 524304 | tf_op jit(solution)/shard_map/psum | solution.py:87
  293.1 23.0 %all-gather.13 = f32[16,1,256]{2,1,0:T(1,128)S(1)} all-gather(f32[1,1,256]{2,1,0:T(1,128)S(1)} %bitcast.368), channel_id=6, replica_groups=mesh['section'=2,'req'=16,'head'=8] {'req'}, dimensions={0}, use_global_device_ids=true | all-gather | bytes 17408 | tf_op jit(solution)/shard_map/all_gather | solution.py:22
  316.8 5.0 fusion.57
  321.9 77.9 %reduce-scatter.7.cloned.1.call-done = f32[16,3584]{1,0:T(8,128)} async-done(((f32[256,3584]{1,0:T(8,128)}), f32[16,3584]{1,0:T(8,128)}) %reduce-scatter.7.cloned.1.call-update) | async-done | bytes 229392 | tf_op jit(solution)/shard_map/reduce_scatter | solution.py:78
  400.9 17.5 %all_to_all.49 = bf16[16,16,1792]{2,1,0:T(8,128)(2,1)S(1)} all-to-all(bf16[16,16,1792]{2,1,0:T(8,128)(2,1)S(1)} %tile.24), channel_id=1, replica_groups=mesh['section'=2,'req'=16,'head'=8] {'req'}, dimensions={0} | all-to-all | bytes 1835008 | tf_op jit(solution)/shard_map/all_to_all | solution.py:18
  418.4 1.4 fusion.14
  419.9 73.1 %all-reduce.7.cloned.1.call-done = f32[256,512]{1,0:T(8,128)} async-done(((f32[256,512]{1,0:T(8,128)}), f32[256,512]{1,0:T(8,128)}) %all-reduce.7.cloned.1.call-update) | async-done | bytes 524304 | tf_op jit(solution)/shard_map/psum | solution.py:87
  493.0 1.9 fusion.41
  494.9 2.0 collective-permute-start
  498.5 23.0 %all-gather.14 = f32[16,1,256]{2,1,0:T(1,128)S(1)} all-gather(f32[1,1,256]{2,1,0:T(1,128)S(1)} %bitcast.366), channel_id=7, replica_groups=mesh['section'=2,'req'=16,'head'=8] {'req'}, dimensions={0}, use_global_device_ids=true | all-gather | bytes 17408 | tf_op jit(solution)/shard_map/all_gather | solution.py:22
  522.2 2.6 fusion.16
  524.8 74.7 %reduce-scatter.9.cloned.1.call-done = f32[16,1280]{1,0:T(8,128)} async-done(((f32[256,1280]{1,0:T(8,128)}), f32[16,1280]{1,0:T(8,128)}) %reduce-scatter.9.cloned.1.call-update) | async-done | bytes 81936 | tf_op jit(solution)/shard_map/reduce_scatter | solution.py:78
  602.2 5.7 all-to-all-start.3
  608.3 1.5 select_reduce_fusion
  609.9 4.3 all-to-all-done.3
  614.2 1.7 select_reduce_fusion.2
  616.1 1.5 fusion.32
  617.6 21.7 %all-gather.15 = f32[16,2,8]{2,1,0:T(2,128)S(1)} all-gather(f32[1,2,8]{2,1,0:T(2,128)S(1)} %bitcast.356), channel_id=8, replica_groups=mesh['section'=2,'req'=16,'head'=8] {'req'}, dimensions={0}, use_global_device_ids=true | all-gather | bytes 1088 | tf_op jit(solution)/shard_map/all_gather | solution.py:22
  639.3 21.4 %all-gather.16 = f32[16,2,8]{2,1,0:T(2,128)S(1)} all-gather(f32[1,2,8]{2,1,0:T(2,128)S(1)} %bitcast.364), channel_id=9, replica_groups=mesh['section'=2,'req'=16,'head'=8] {'req'}, dimensions={0}, use_global_device_ids=true | all-gather | bytes 1088 | tf_op jit(solution)/shard_map/all_gather | solution.py:22
  660.8 24.0 %all-gather.8 = f32[32,8,128]{2,1,0:T(8,128)S(1)} all-gather(f32[2,8,128]{2,1,0:T(8,128)S(1)} %fusion.32), channel_id=10, replica_groups=mesh['section'=2,'req'=16,'head'=8] {'req'}, dimensions={0}, use_global_device_ids=true | all-gather | bytes 139264 | tf_op jit(solution)/shard_map/all_gather | solution.py:22
  684.7 1.7 while.102
  687.1 1.6 fusion.26
  688.7 13.1 %all_to_all.50 = bf16[16,16,1024]{2,1,0:T(8,128)(2,1)S(1)} all-to-all(bf16[16,16,1024]{2,1,0:T(8,128)(2,1)S(1)} %tile.54), channel_id=1, replica_groups=mesh['section'=2,'req'=16,'head'=8] {'req'}, dimensions={0} | all-to-all | bytes 1048576 | tf_op jit(solution)/shard_map/all_to_all | solution.py:18
  701.8 1.3 fusion.28
  703.2 73.2 %all-reduce.9.cloned.1.call-done = f32[256,512]{1,0:T(8,128)} async-done(((f32[256,512]{1,0:T(8,128)}), f32[256,512]{1,0:T(8,128)}) %all-reduce.9.cloned.1.call-update) | async-done | bytes 524304 | tf_op jit(solution)/shard_map/psum | solution.py:87
  777.5 23.0 %all-gather.17 = f32[16,1,256]{2,1,0:T(1,128)S(1)} all-gather(f32[1,1,256]{2,1,0:T(1,128)S(1)} %bitcast.367), channel_id=11, replica_groups=mesh['section'=2,'req'=16,'head'=8] {'req'}, dimensions={0}, use_global_device_ids=true | all-gather | bytes 17408 | tf_op jit(solution)/shard_map/all_gather | solution.py:22
  801.3 5.0 fusion.54
  806.4 77.7 %reduce-scatter.11.cloned.1.call-done = f32[16,3584]{1,0:T(8,128)} async-done(((f32[256,3584]{1,0:T(8,128)}), f32[16,3584]{1,0:T(8,128)}) %reduce-scatter.11.cloned.1.call-update) | async-done | bytes 229392 | tf_op jit(solution)/shard_map/reduce_scatter | solution.py:78
  885.2 17.5 %all_to_all.51 = bf16[16,16,1792]{2,1,0:T(8,128)(2,1)S(1)} all-to-all(bf16[16,16,1792]{2,1,0:T(8,128)(2,1)S(1)} %tile.55), channel_id=1, replica_groups=mesh['section'=2,'req'=16,'head'=8] {'req'}, dimensions={0} | all-to-all | bytes 1835008 | tf_op jit(solution)/shard_map/all_to_all | solution.py:18
  902.7 1.4 fusion.12
  904.2 73.2 %all-reduce.11.cloned.1.call-done = f32[256,512]{1,0:T(8,128)} async-done(((f32[256,512]{1,0:T(8,128)}), f32[256,512]{1,0:T(8,128)}) %all-reduce.11.cloned.1.call-update) | async-done | bytes 524304 | tf_op jit(solution)/shard_map/psum | solution.py:87
  977.4 1.9 fusion.53
  (363 shorter events, 25.1 us)
Async XLA Ops:
  6.5 411.9 %copy-start = (bf16[1,1792,512]{2,1,0:T(8,128)(2,1)S(1)}, bf16[1,1792,512]{2,1,0:T(8,128)(2,1)}, u32[]{:S(2)}) copy-start(bf16[1,1792,512]{2,1,0:T(8,128)(2,1)} %param.29) | copy-start | bytes 5505028
  6.5 108.0 %reduce-scatter.5.cloned.1.call-start = ((), (), s32[]{:S(2)}) async-start(), calls=%async_computation.10 | async-start | bytes 1392640 | tf_op jit(solution)/shard_map/reduce_scatter | solution.py:78
  32.5 3.1 copy-start.8
  32.5 3.6 copy-start.9
  117.9 11.9 %all-to-all-start = ((bf16[16,2,512]{2,1,0:T(2,128)(2,1)}), bf16[16,2,512]{2,1,0:T(2,128)(2,1)S(1)}, u32[]{:S(2)}, u32[]{:S(2)}) async-start(bf16[16,2,512]{2,1,0:T(2,128)(2,1)} %reshape.857), calls=%async_computation.1 | async-start | bytes 65536 | tf_op jit(solution)/shard_map/all_to_all | solution.py:18
  123.6 168.3 %all-reduce.5.cloned.1.call-start = ((), (), s32[]{:S(2)}) async-start(), calls=%async_computation.11 | async-start | bytes 1048576 | tf_op jit(solution)/shard_map/psum | solution.py:87
  202.6 14.8 %copy-start.3 = (bf16[1,1,1024,512]{3,2,1,0:T(8,128)(2,1)S(1)}, bf16[1,1,1024,512]{3,2,1,0:T(8,128)(2,1)}, u32[]{:S(2)}) copy-start(bf16[1,1,1024,512]{3,2,1,0:T(8,128)(2,1)} %param.26) | copy-start | bytes 3145732
  218.6 181.2 %reduce-scatter.7.cloned.1.call-start = ((), (), s32[]{:S(2)}) async-start(), calls=%async_computation.12 | async-start | bytes 3899392 | tf_op jit(solution)/shard_map/reduce_scatter | solution.py:78
  218.7 4.5 copy-start.7
  218.7 73.2 %copy-start.2 = (bf16[256,512]{1,0:T(8,128)(2,1)S(1)}, bf16[256,512]{1,0:T(8,128)(2,1)}, u32[]{:S(2)}) copy-start(bf16[256,512]{1,0:T(8,128)(2,1)} %param.23) | copy-start | bytes 786436
  293.1 28.8 %copy-start.5 = (bf16[256,512]{1,0:T(8,128)(2,1)}, bf16[256,512]{1,0:T(8,128)(2,1)S(1)}, u32[]{:S(2)}) copy-start(bf16[256,512]{1,0:T(8,128)(2,1)S(1)} %get-tuple-element.863) | copy-start | bytes 786436
  321.9 171.1 %all-reduce.7.cloned.1.call-start = ((), (), s32[]{:S(2)}) async-start(), calls=%async_computation.13 | async-start | bytes 1048576 | tf_op jit(solution)/shard_map/psum | solution.py:87
  419.8 102.4 %copy-start.1 = (bf16[1,512,1,1280]{3,1,2,0:T(8,128)(2,1)S(1)}, bf16[1,512,1,1280]{3,1,2,0:T(8,128)(2,1)}, u32[]{:S(2)}) copy-start(bf16[1,512,1,1280]{3,1,2,0:T(8,128)(2,1)} %param.25) | copy-start | bytes 3932164
  419.8 179.7 %reduce-scatter.9.cloned.1.call-start = ((), (), s32[]{:S(2)}) async-start(), calls=%async_computation.14 | async-start | bytes 1392640 | tf_op jit(solution)/shard_map/reduce_scatter | solution.py:78
  494.9 2.8 collective-permute-start
  602.2 11.9 %all-to-all-start.3 = ((bf16[16,2,512]{2,1,0:T(2,128)(2,1)}), bf16[16,2,512]{2,1,0:T(2,128)(2,1)S(1)}, u32[]{:S(2)}, u32[]{:S(2)}) async-start(bf16[16,2,512]{2,1,0:T(2,128)(2,1)} %reshape.859), calls=%async_computation.6 | async-start | bytes 65536 | tf_op jit(solution)/shard_map/all_to_all | solution.py:18
  607.9 168.5 %all-reduce.9.cloned.1.call-start = ((), (), s32[]{:S(2)}) async-start(), calls=%async_computation.15 | async-start | bytes 1048576 | tf_op jit(solution)/shard_map/psum | solution.py:87
  687.1 14.8 %copy-start.4 = (bf16[1,1,1024,512]{3,2,1,0:T(8,128)(2,1)S(1)}, bf16[1,1,1024,512]{3,2,1,0:T(8,128)(2,1)}, u32[]{:S(2)}) copy-start(bf16[1,1,1024,512]{3,2,1,0:T(8,128)(2,1)} %param.26) | copy-start | bytes 3145732
  688.7 87.7 %copy-start.6 = (bf16[256,512]{1,0:T(8,128)(2,1)S(1)}, bf16[256,512]{1,0:T(8,128)(2,1)}, u32[]{:S(2)}) copy-start(bf16[256,512]{1,0:T(8,128)(2,1)} %get-tuple-element.861) | copy-start | bytes 786436
  703.1 181.0 %reduce-scatter.11.cloned.1.call-start = ((), (), s32[]{:S(2)}) async-start(), calls=%async_computation.16 | async-start | bytes 3899392 | tf_op jit(solution)/shard_map/reduce_scatter | solution.py:78
  806.3 171.0 %all-reduce.11.cloned.1.call-start = ((), (), s32[]{:S(2)}) async-start(), calls=%async_computation.17 | async-start | bytes 1048576 | tf_op jit(solution)/shard_map/psum | solution.py:87
Sparse Core Ops, SparseCore 0:
  35.7 78.7 reduce-scatter.4
  218.7 73.0 all-reduce.4
  322.0 77.7 reduce-scatter.6
  420.0 73.0 all-reduce.6
  524.9 74.5 reduce-scatter.8
  703.2 73.0 all-reduce.8
  806.5 77.6 reduce-scatter.10
  904.3 73.0 all-reduce.10
